TPU v7x, 32 devices: a whole 2x2x4 slice. The times are simulated.
32 devices in a mesh: rows: 16 (over z, y, x), rep: 2 (over core).
Axes of the slice: x: 2, y: 2, z: 4, core: 2. Of those that a mesh axis runs over, the one named last changes fastest.
Arguments:
- grad_out: bfloat16 [2048, 1024], P('rows'), may hold values from -8 to 8
- w_self: bfloat16 [1024, 1024], replicated, may hold values from -0.1875 to 0.1875
- w_neigh: bfloat16 [1024, 1024], replicated, may hold values from -0.1875 to 0.1875
- adj_tiles: bfloat16 [16, 8, 128, 128], P('rows'), may hold values from -0.3125 to 0.3125
- tile_index: int32 [16, 8], P('rows'), may hold values from 0 to 15, as said below
- tile_count: int32 [16], P('rows'), may hold values from 4 to 8, as said below
- prompt_ids: int32 [2048], P('rows'), may hold values from 0 to 15
Outputs:
- input_grad: bfloat16 [2048, 1024], P('rows')
- prompt_grad: float32 [16, 1024], replicated
Inputs may be any that keep to these rules, and one draw needn't show every extreme that they name: `tile_index`: each row holds 8 different tile numbers; only the first tile_count entries of a row are used. `tile_count`: some destination tile uses all 8 slots.
All inputs are finite; a program needn't handle non-finite values.
Results may differ from a plain program's by a relative error of at most 0.0041.
Values may be sent and summed in bfloat16 or wider, within the bound.
A program may use at most 64 MiB of HBM per device.

v0:
```python
import math
import jax
import jax.numpy as jnp
from jax import lax
from jax.sharding import PartitionSpec as P

PROMPTS = 16


def shards(grad_out, w_self, w_neigh, adj_tiles, tile_index, tile_count, prompt_ids):
    rows_dev, width = grad_out.shape
    local_tiles, max_slots, tile_size, _ = adj_tiles.shape
    n_rows = lax.axis_size("rows")
    n_rep = lax.axis_size("rep")
    rep_index = lax.axis_index("rep")
    total_tiles = local_tiles * n_rows
    slot_ids = jnp.arange(max_slots)
    in_use = slot_ids[None, :] < tile_count[:, None]
    matches = (tile_index[:, :, None] == jnp.arange(total_tiles)[None, None, :]) & in_use[
        :, :, None
    ]
    present = jnp.any(matches, axis=1)
    slot_table = jnp.argmax(matches, axis=1)
    contract = (((1,), (1,)), ((), ()))
    half_rows = rows_dev // n_rep
    mine = lax.dynamic_slice_in_dim(grad_out, rep_index * half_rows, half_rows, 0)
    initial = jnp.zeros((local_tiles, tile_size, width), jnp.float32)

    def half_column(place):
        return place // half_rows * rows_dev + rep_index * half_rows + place % half_rows

    piece = lax.all_gather(mine, "rows", axis=0, tiled=True)
    piece_rows = piece.shape[0]
    unit = math.gcd(math.gcd(piece_rows, tile_size), half_rows)
    segments = piece_rows // unit
    feat = piece.shape[1]

    def one_segment(index, carry):
        start = index * unit
        rows_part = lax.dynamic_slice_in_dim(piece, start, unit, 0)
        column = half_column(start)
        source = column // tile_size
        offset = column % tile_size
        slot = slot_table[0, source]
        zero = jnp.zeros((), jnp.int32)
        block = lax.dynamic_slice(
            adj_tiles, (jnp.int32(0), slot, zero, offset), (1, 1, tile_size, unit)
        )
        block = block.reshape(tile_size, unit)

        def product(args):
            blk, part_rows = args
            return jnp.dot(blk, part_rows, preferred_element_type=jnp.float32)

        def nothing(args):
            return jnp.zeros((tile_size, feat), jnp.float32)

        term = lax.cond(present[0, source], product, nothing, (block, rows_part))
        updated = [carry[0] + term]
        return jnp.stack(updated, axis=0)

    partial_value = lax.fori_loop(0, segments, one_segment, initial)
    summed = lax.psum(partial_value.reshape(rows_dev, width), "rep")
    aggregate = summed.astype(jnp.bfloat16)
    full_grad = lax.dot_general(grad_out, w_self, contract, preferred_element_type=jnp.float32)
    full_grad = full_grad + lax.dot_general(
        aggregate, w_neigh, contract, preferred_element_type=jnp.float32
    )
    onehot = (prompt_ids[None, :] == jnp.arange(PROMPTS)[:, None]).astype(jnp.float32)
    prompt_part = jnp.dot(onehot, full_grad, precision=lax.Precision.HIGHEST)
    prompt_grad = lax.psum(prompt_part, "rows")
    return (full_grad.astype(jnp.bfloat16), prompt_grad)


def solution(mesh):
    placed = (
        P("rows", None),
        P(),
        P(),
        P("rows", None, None, None),
        P("rows", None),
        P("rows"),
        P("rows"),
    )
    return jax.shard_map(
        shards, mesh=mesh, in_specs=placed, out_specs=(P("rows", None), P()), check_vma=False
    )
```

profile of v0, /device:TPU:0, one launch (start us, length us, event | category | flops | bytes accessed | tf_op | source)
XLA Modules:
  0.0 249.7 jit_solution(9167569189331557641)
XLA Ops:
  7.2 1.7 constant_dynamic-slice_fusion.2
  10.4 1.3 iota_reduce_fusion
  11.7 3.3 %fusion.13 = f32[128,1024]{1,0:T(8,128)} fusion(bf16[128,1024]{1,0:T(8,128)(2,1)} %param.11, bf16[1024,1024]{1,0:T(8,128)(2,1)} %param.12), kind=kOutput, calls=%fused_computation.22 | convolution fusion | flops 268435456 | bytes 2883584 | tf_op jit(solution)/shard_map/dot_general | solution.py:65
  15.0 59.5 %all-gather.2.cloned.1.call-done = bf16[1024,1024]{1,0:T(8,128)(2,1)} async-done(((bf16[64,1024]{1,0:T(8,128)(2,1)}), bf16[1024,1024]{1,0:T(8,128)(2,1)}) %all-gather.2.cloned.1.call-update) | async-done | bytes 2097168 | tf_op jit(solution)/shard_map/all_gather | solution.py:32
  74.5 45.9 %while.16 = (s32[]{:T(128)}, f32[1,128,1024]{2,1,0:T(8,128)S(1)}, s32[]{:T(128)}, pred[1,16]{1,0:T(4,128)(4,1)S(1)}, s32[1,16]{1,0:T(1,128)S(1)}, /*index=5*/bf1...) while((s32[]{:T(128)}, f32[1,128,1024]{2,1,0:T(8,128)S(1)}, ...), condition=%wide.region_5.6_spmd, body=%wide.region_2.5_spmd.sunk | while | flops 16908344 | bytes 2261804 | solution.py:62
  75.3 4.7 %conditional.2 = (f32[128,1024]{1,0:T(8,128)S(1)}) conditional(s32[]{:T(128)} %bitcast.25, () %tuple.66, (s32[1,16]{1,0:T(1,128)S(1)}, s32[]{:T(128)}, s32[]{:T(128)}, bf16[1,8,128,128]{3,2,1,0:T(8,128)(2,1)}, s32[]{:T(128)}, /*index=5*/pred[]{:T(512)}, bf16[1024,1024]{1,0:T(8,128)(2,1)}) %tuple.67), branch_computations={%region_3.3_spmd, %region_4.4_spmd} | conditional | flops 16777228 | bytes 688299 | solution.py:58
  78.7 1.2 fusion
  80.8 4.7 %conditional.2 = (f32[128,1024]{1,0:T(8,128)S(1)}) conditional(s32[]{:T(128)} %bitcast.25, () %tuple.66, (s32[1,16]{1,0:T(1,128)S(1)}, s32[]{:T(128)}, s32[]{:T(128)}, bf16[1,8,128,128]{3,2,1,0:T(8,128)(2,1)}, s32[]{:T(128)}, /*index=5*/pred[]{:T(512)}, bf16[1024,1024]{1,0:T(8,128)(2,1)}) %tuple.67), branch_computations={%region_3.3_spmd, %region_4.4_spmd} | conditional | flops 16777228 | bytes 688299 | solution.py:58
  84.3 1.2 fusion
  86.4 0.8 conditional.2
  88.0 0.8 conditional.2
  89.7 0.8 conditional.2
  91.3 4.7 %conditional.2 = (f32[128,1024]{1,0:T(8,128)S(1)}) conditional(s32[]{:T(128)} %bitcast.25, () %tuple.66, (s32[1,16]{1,0:T(1,128)S(1)}, s32[]{:T(128)}, s32[]{:T(128)}, bf16[1,8,128,128]{3,2,1,0:T(8,128)(2,1)}, s32[]{:T(128)}, /*index=5*/pred[]{:T(512)}, bf16[1024,1024]{1,0:T(8,128)(2,1)}) %tuple.67), branch_computations={%region_3.3_spmd, %region_4.4_spmd} | conditional | flops 16777228 | bytes 688299 | solution.py:58
  94.8 1.2 fusion
  96.9 4.7 %conditional.2 = (f32[128,1024]{1,0:T(8,128)S(1)}) conditional(s32[]{:T(128)} %bitcast.25, () %tuple.66, (s32[1,16]{1,0:T(1,128)S(1)}, s32[]{:T(128)}, s32[]{:T(128)}, bf16[1,8,128,128]{3,2,1,0:T(8,128)(2,1)}, s32[]{:T(128)}, /*index=5*/pred[]{:T(512)}, bf16[1024,1024]{1,0:T(8,128)(2,1)}) %tuple.67), branch_computations={%region_3.3_spmd, %region_4.4_spmd} | conditional | flops 16777228 | bytes 688299 | solution.py:58
  100.3 1.2 fusion
  107.3 4.7 %conditional.2 = (f32[128,1024]{1,0:T(8,128)S(1)}) conditional(s32[]{:T(128)} %bitcast.25, () %tuple.66, (s32[1,16]{1,0:T(1,128)S(1)}, s32[]{:T(128)}, s32[]{:T(128)}, bf16[1,8,128,128]{3,2,1,0:T(8,128)(2,1)}, s32[]{:T(128)}, /*index=5*/pred[]{:T(512)}, bf16[1024,1024]{1,0:T(8,128)(2,1)}) %tuple.67), branch_computations={%region_3.3_spmd, %region_4.4_spmd} | conditional | flops 16777228 | bytes 688299 | solution.py:58
  110.8 1.2 fusion
  112.9 0.8 conditional.2
  120.4 4.8 %all-reduce.4 = bf16[128,1024]{1,0:T(8,128)(2,1)S(1)} all-reduce(f32[128,1024]{1,0:T(8,128)S(1)} %bitcast.27), channel_id=1, replica_groups=mesh['rows'=16,'rep'=2] {'rep'}, use_global_device_ids=true, to_apply=%region_6.7 | all-reduce | flops 131072 | bytes 786432 | tf_op jit(solution)/shard_map/psum | solution.py:63
  125.2 2.6 %fusion.12 = (bf16[128,1024]{1,0:T(8,128)(2,1)}, f32[128,1024]{1,0:T(8,128)S(1)}) fusion(f32[128,1024]{1,0:T(8,128)} %fusion.13, bf16[128,1024]{1,0:T(8,128)(2,1)S(1)} %all-reduce.4, bf16[1024,1024]{1,0:T(8,128)(2,1)S(1)} %copy-done), kind=kOutput, calls=%fused_computation.21 | convolution fusion | flops 268697600 | bytes 3670016 | tf_op jit(solution)/shard_map/dot_general | solution.py:66
  127.8 0.9 fusion.7
  128.8 112.6 %all-reduce.3.cloned.1.call-done = f32[16,1024]{1,0:T(8,128)} async-done(((f32[16,1024]{1,0:T(8,128)}), f32[16,1024]{1,0:T(8,128)}) %all-reduce.3.cloned.1.call-update) | async-done | bytes 65552 | tf_op jit(solution)/shard_map/psum | solution.py:71
  241.4 1.5 copy.21
  (66 shorter events, 22.8 us)
Async XLA Ops:
  7.2 118.1 %copy-start = (bf16[1024,1024]{1,0:T(8,128)(2,1)S(1)}, bf16[1024,1024]{1,0:T(8,128)(2,1)}, u32[]{:S(2)}) copy-start(bf16[1024,1024]{1,0:T(8,128)(2,1)} %param.13) | copy-start | bytes 6291460
  7.2 67.3 %all-gather.2.cloned.1.call-start = ((), (), s32[]{:S(2)}) async-start(), calls=%async_computation | async-start | bytes 2228224 | tf_op jit(solution)/shard_map/all_gather | solution.py:32
  9.0 232.4 %all-reduce.3.cloned.1.call-start = ((), (), s32[]{:S(2)}) async-start(), calls=%async_computation.1 | async-start | bytes 131072 | tf_op jit(solution)/shard_map/psum | solution.py:71
  120.4 7.4 %copy-start.1 = (s32[128]{0:T(128)S(1)}, s32[128]{0:T(128)}, u32[]{:S(2)}) copy-start(s32[128]{0:T(128)} %param.17) | copy-start | bytes 1540
Sparse Core Ops, SparseCore 0:
  11.3 63.0 all-gather.1
  128.9 112.4 all-reduce.2
where the time goes:
time: 250 us
  waiting for transfers between devices  172 us (69%)
  loops' own time  23.3 us (9%)
  other arithmetic  14.8 us (6%)
  between operations  14.7 us (6%)
  matrix products  12.8 us (5%)
  local copies, waits for them, and re-layouts  7.06 us (3%)
  blocking collectives  4.82 us (2%)
    psum x1, waiting for transfers between devices, shards(): prompt_grad = lax.psum(prompt_part, 'rows')  113 us
    all_gather x1, waiting for transfers between devices, shards(): piece = lax.all_gather(mine, 'rows', axis=0, tiled=True)  59.5 us
    another operation x16, loops' own time, one_segment(): term = lax.cond(present[0, source], product, nothing, (block, rows_part))  21.9 us
    convert_element_type x16, other arithmetic, one_segment(): term = lax.cond(present[0, source], product, nothing, (block, rows_part))  10.6 us
    dot_general x5, matrix products, product(): return jnp.dot(blk, part_rows, preferred_element_type=jnp.float32)  5.96 us
  transfers between devices with their start and end apart: 2, of which 2 were waited for; matrix products, arithmetic and copies ran while one was open for 2% of the time, Pallas kernels for 0%

commit v1 on v0

--- a/solution.py
+++ b/solution.py
@@ -3,8 +3,19 @@
 import jax.numpy as jnp
 from jax import lax
 from jax.sharding import PartitionSpec as P
+from jax.lax import axis_size, ppermute
 
 PROMPTS = 16
+
+
+def lead_ports(piece_in):
+    cores_n = axis_size("rows")
+    y2, block_last = (piece_in, 0)
+    while 1 << block_last < cores_n:
+        found_now = ppermute(y2, "rows", [(kk, kk ^ 1 << block_last) for kk in range(cores_n)])
+        y2 = y2 + found_now
+        block_last = block_last + 1
+    return y2
 
 
 def shards(grad_out, w_self, w_neigh, adj_tiles, tile_index, tile_count, prompt_ids):
@@ -68,7 +79,7 @@
     )
     onehot = (prompt_ids[None, :] == jnp.arange(PROMPTS)[:, None]).astype(jnp.float32)
     prompt_part = jnp.dot(onehot, full_grad, precision=lax.Precision.HIGHEST)
-    prompt_grad = lax.psum(prompt_part, "rows")
+    prompt_grad = lead_ports(prompt_part)
     return (full_grad.astype(jnp.bfloat16), prompt_grad)
 
 

time: 250 us -> 165 us (0.66)
  waiting for transfers between devices: 172 us -> 75.7 us
  starting transfers between devices: 0.08 us -> 12.3 us
    psum x1 -> x0, waiting for transfers between devices: 113 us -> none  [shards(): prompt_grad = lax.psum(prompt_part, 'rows')]
    ppermute x0 -> x4, waiting for transfers between devices: none -> 16.1 us  [lead_ports(): ppermute(y2, 'rows', [(kk, kk ^ 1 << block_last) for kk in range(cores_n)])]
    ppermute x0 -> x4, starting transfers between devices: none -> 12.3 us  [lead_ports(): ppermute(y2, 'rows', [(kk, kk ^ 1 << block_last) for kk in range(cores_n)])]
  transfers between devices with their start and end apart: 2 -> 5, of which waited for: 2 -> 5; matrix products, arithmetic and copies ran while one was open for 2% -> 3% of each run, Pallas kernels for 0% -> 0%
where the time goes in v1:
time: 165 us; the launch traced here: 164 us
  waiting for transfers between devices  75.7 us (46%)
  loops' own time  23.3 us (14%)
  other arithmetic  15.4 us (9%)
  between operations  14.8 us (9%)
  starting transfers between devices  12.3 us (7%)
  matrix products  12.2 us (7%)
  local copies, waits for them, and re-layouts  5.59 us (3%)
  blocking collectives  4.82 us (3%)
    all_gather x1, waiting for transfers between devices, shards(): piece = lax.all_gather(mine, 'rows', axis=0, tiled=True)  59.5 us
    another operation x16, loops' own time, one_segment(): term = lax.cond(present[0, source], product, nothing, (block, rows_part))  21.9 us
    ppermute x4, waiting for transfers between devices, lead_ports(): ppermute(y2, 'rows', [(kk, kk ^ 1 << block_last) for kk in range(cores_n)])  16.1 us
    ppermute x4, starting transfers between devices, lead_ports(): ppermute(y2, 'rows', [(kk, kk ^ 1 << block_last) for kk in range(cores_n)])  12.3 us
    convert_element_type x16, other arithmetic, one_segment(): term = lax.cond(present[0, source], product, nothing, (block, rows_part))  10.6 us
    dot_general x5, matrix products, product(): return jnp.dot(blk, part_rows, preferred_element_type=jnp.float32)  5.96 us
    psum x1, blocking collectives, shards(): summed = lax.psum(partial_value.reshape(rows_dev, width), 'rep')  4.82 us
    dynamic_slice x5, local copies, waits for them, and re-layouts, one_segment(): slot = slot_table[0, source]  3.34 us
  transfers between devices with their start and end apart: 5, of which 5 were waited for; matrix products, arithmetic and copies ran while one was open for 3% of the time, Pallas kernels for 0%

profile of v1, /device:TPU:0, one launch (start us, length us, event | category | flops | bytes accessed | tf_op | source)
XLA Modules:
  0.0 164.1 jit_solution(10900259326293556968)
XLA Ops:
  7.2 1.7 %constant_dynamic-slice_fusion.2 = bf16[64,1024]{1,0:T(8,128)(2,1)} fusion(bf16[128,1024]{1,0:T(8,128)(2,1)} %param.11, s32[]{:T(128)S(6)} %select_n.120), kind=kLoop, calls=%fused_computation.19 | loop fusion | bytes 262148 | tf_op jit(solution)/shard_map/dynamic_slice | solution.py:37
  10.4 1.3 iota_reduce_fusion
  11.6 3.3 %fusion.13 = f32[128,1024]{1,0:T(8,128)} fusion(bf16[128,1024]{1,0:T(8,128)(2,1)} %param.11, bf16[1024,1024]{1,0:T(8,128)(2,1)} %param.12), kind=kOutput, calls=%fused_computation.22 | convolution fusion | flops 268435456 | bytes 2883584 | tf_op jit(solution)/shard_map/dot_general | solution.py:76
  15.0 59.5 %all-gather.2.cloned.1.call-done = bf16[1024,1024]{1,0:T(8,128)(2,1)} async-done(((bf16[64,1024]{1,0:T(8,128)(2,1)}), bf16[1024,1024]{1,0:T(8,128)(2,1)}) %all-gather.2.cloned.1.call-update) | async-done | bytes 2097168 | tf_op jit(solution)/shard_map/all_gather | solution.py:43
  74.5 45.9 %while.16 = (s32[]{:T(128)}, f32[1,128,1024]{2,1,0:T(8,128)S(1)}, s32[]{:T(128)}, pred[1,16]{1,0:T(4,128)(4,1)S(1)}, s32[1,16]{1,0:T(1,128)S(1)}, /*index=5*/bf1...) while((s32[]{:T(128)}, f32[1,128,1024]{2,1,0:T(8,128)S(1)}, ...), condition=%wide.region_5.6_spmd, body=%wide.region_2.5_spmd.sunk | while | flops 16908344 | bytes 2261804 | solution.py:73
  75.3 4.7 %conditional.2 = (f32[128,1024]{1,0:T(8,128)S(1)}) conditional(s32[]{:T(128)} %bitcast.25, () %tuple.66, (s32[1,16]{1,0:T(1,128)S(1)}, s32[]{:T(128)}, s32[]{:T(128)}, bf16[1,8,128,128]{3,2,1,0:T(8,128)(2,1)}, s32[]{:T(128)}, /*index=5*/pred[]{:T(512)}, bf16[1024,1024]{1,0:T(8,128)(2,1)}) %tuple.67), branch_computations={%region_3.3_spmd, %region_4.4_spmd} | conditional | flops 16777228 | bytes 688299 | solution.py:69
  78.7 1.2 fusion
  80.8 4.7 %conditional.2 = (f32[128,1024]{1,0:T(8,128)S(1)}) conditional(s32[]{:T(128)} %bitcast.25, () %tuple.66, (s32[1,16]{1,0:T(1,128)S(1)}, s32[]{:T(128)}, s32[]{:T(128)}, bf16[1,8,128,128]{3,2,1,0:T(8,128)(2,1)}, s32[]{:T(128)}, /*index=5*/pred[]{:T(512)}, bf16[1024,1024]{1,0:T(8,128)(2,1)}) %tuple.67), branch_computations={%region_3.3_spmd, %region_4.4_spmd} | conditional | flops 16777228 | bytes 688299 | solution.py:69
  84.3 1.2 fusion
  88.0 0.8 conditional.2
  89.7 0.8 conditional.2
  91.3 4.7 %conditional.2 = (f32[128,1024]{1,0:T(8,128)S(1)}) conditional(s32[]{:T(128)} %bitcast.25, () %tuple.66, (s32[1,16]{1,0:T(1,128)S(1)}, s32[]{:T(128)}, s32[]{:T(128)}, bf16[1,8,128,128]{3,2,1,0:T(8,128)(2,1)}, s32[]{:T(128)}, /*index=5*/pred[]{:T(512)}, bf16[1024,1024]{1,0:T(8,128)(2,1)}) %tuple.67), branch_computations={%region_3.3_spmd, %region_4.4_spmd} | conditional | flops 16777228 | bytes 688299 | solution.py:69
  94.8 1.2 fusion
  96.9 4.7 %conditional.2 = (f32[128,1024]{1,0:T(8,128)S(1)}) conditional(s32[]{:T(128)} %bitcast.25, () %tuple.66, (s32[1,16]{1,0:T(1,128)S(1)}, s32[]{:T(128)}, s32[]{:T(128)}, bf16[1,8,128,128]{3,2,1,0:T(8,128)(2,1)}, s32[]{:T(128)}, /*index=5*/pred[]{:T(512)}, bf16[1024,1024]{1,0:T(8,128)(2,1)}) %tuple.67), branch_computations={%region_3.3_spmd, %region_4.4_spmd} | conditional | flops 16777228 | bytes 688299 | solution.py:69
  100.3 1.2 fusion
  107.3 4.7 %conditional.2 = (f32[128,1024]{1,0:T(8,128)S(1)}) conditional(s32[]{:T(128)} %bitcast.25, () %tuple.66, (s32[1,16]{1,0:T(1,128)S(1)}, s32[]{:T(128)}, s32[]{:T(128)}, bf16[1,8,128,128]{3,2,1,0:T(8,128)(2,1)}, s32[]{:T(128)}, /*index=5*/pred[]{:T(512)}, bf16[1024,1024]{1,0:T(8,128)(2,1)}) %tuple.67), branch_computations={%region_3.3_spmd, %region_4.4_spmd} | conditional | flops 16777228 | bytes 688299 | solution.py:69
  110.8 1.2 fusion
  120.4 4.8 %all-reduce.1 = bf16[128,1024]{1,0:T(8,128)(2,1)S(1)} all-reduce(f32[128,1024]{1,0:T(8,128)S(1)} %bitcast.27), channel_id=1, replica_groups=mesh['rows'=16,'rep'=2] {'rep'}, use_global_device_ids=true, to_apply=%region_6.7 | all-reduce | flops 131072 | bytes 786432 | tf_op jit(solution)/shard_map/psum | solution.py:74
  125.2 2.6 %fusion.12 = (bf16[128,1024]{1,0:T(8,128)(2,1)}, f32[128,1024]{1,0:T(8,128)S(1)}) fusion(f32[128,1024]{1,0:T(8,128)} %fusion.13, bf16[128,1024]{1,0:T(8,128)(2,1)S(1)} %all-reduce.1, bf16[1024,1024]{1,0:T(8,128)(2,1)S(1)} %copy-done), kind=kOutput, calls=%fused_computation.21 | convolution fusion | flops 268697600 | bytes 3670016 | tf_op jit(solution)/shard_map/dot_general | solution.py:77
  128.2 4.4 %collective-permute-done = f32[16,1024]{1,0:T(8,128)S(1)} collective-permute-done((f32[16,1024]{1,0:T(8,128)S(1)}, f32[16,1024]{1,0:T(8,128)S(1)}, u32[]{:S(2)}, u32[]{:S(2)}) %collective-permute-start) | collective-permute-done | bytes 65568 | tf_op jit(solution)/shard_map/ppermute | solution.py:15
  132.6 12.1 %collective-permute-start.1 = (f32[16,1024]{1,0:T(8,128)S(1)}, f32[16,1024]{1,0:T(8,128)S(1)}, u32[]{:S(2)}, u32[]{:S(2)}) collective-permute-start(f32[16,1024]{1,0:T(8,128)S(1)} %add.160), channel_id=1, source_target_pairs={{0,4},{2,6},{4,0},{6,2},{8,12},{10,14},{12,8},{14,10},{16,20},{18,... | collective-permute-start | bytes 196616 | tf_op jit(solution)/shard_map/ppermute | solution.py:15
  144.7 2.2 %collective-permute-done.1 = f32[16,1024]{1,0:T(8,128)S(1)} collective-permute-done((f32[16,1024]{1,0:T(8,128)S(1)}, f32[16,1024]{1,0:T(8,128)S(1)}, u32[]{:S(2)}, u32[]{:S(2)}) %collective-permute-start.1) | collective-permute-done | bytes 65568 | tf_op jit(solution)/shard_map/ppermute | solution.py:15
  147.0 4.3 %collective-permute-done.2 = f32[16,1024]{1,0:T(8,128)S(1)} collective-permute-done((f32[16,1024]{1,0:T(8,128)S(1)}, f32[16,1024]{1,0:T(8,128)S(1)}, u32[]{:S(2)}, u32[]{:S(2)}) %collective-permute-start.2) | collective-permute-done | bytes 65568 | tf_op jit(solution)/shard_map/ppermute | solution.py:15
  151.3 5.3 %collective-permute-done.3 = f32[16,1024]{1,0:T(8,128)S(1)} collective-permute-done((f32[16,1024]{1,0:T(8,128)S(1)}, f32[16,1024]{1,0:T(8,128)S(1)}, u32[]{:S(2)}, u32[]{:S(2)}) %collective-permute-start.3) | collective-permute-done | bytes 65568 | tf_op jit(solution)/shard_map/ppermute | solution.py:15
  (74 shorter events, 25.4 us)
Async XLA Ops:
  7.2 118.1 %copy-start = (bf16[1024,1024]{1,0:T(8,128)(2,1)S(1)}, bf16[1024,1024]{1,0:T(8,128)(2,1)}, u32[]{:S(2)}) copy-start(bf16[1024,1024]{1,0:T(8,128)(2,1)} %param.13) | copy-start | bytes 6291460
  7.2 67.3 %all-gather.2.cloned.1.call-start = ((), (), s32[]{:S(2)}) async-start(), calls=%async_computation | async-start | bytes 2228224 | tf_op jit(solution)/shard_map/all_gather | solution.py:43
  120.4 7.4 %copy-start.1 = (s32[128]{0:T(128)S(1)}, s32[128]{0:T(128)}, u32[]{:S(2)}) copy-start(s32[128]{0:T(128)} %param.17) | copy-start | bytes 1540
  128.1 4.4 %collective-permute-start = (f32[16,1024]{1,0:T(8,128)S(1)}, f32[16,1024]{1,0:T(8,128)S(1)}, u32[]{:S(2)}, u32[]{:S(2)}) collective-permute-start(f32[16,1024]{1,0:T(8,128)S(1)} %fusion.7), channel_id=1, source_target_pairs={{0,2},{2,0},{4,6},{6,4},{8,10},{10,8},{12,14},{14,12},{16,18},{18,... | collective-permute-start | bytes 196616 | tf_op jit(solution)/shard_map/ppermute | solution.py:15
  132.6 14.3 %collective-permute-start.1 = (f32[16,1024]{1,0:T(8,128)S(1)}, f32[16,1024]{1,0:T(8,128)S(1)}, u32[]{:S(2)}, u32[]{:S(2)}) collective-permute-start(f32[16,1024]{1,0:T(8,128)S(1)} %add.160), channel_id=1, source_target_pairs={{0,4},{2,6},{4,0},{6,2},{8,12},{10,14},{12,8},{14,10},{16,20},{18,... | collective-permute-start | bytes 196616 | tf_op jit(solution)/shard_map/ppermute | solution.py:15
  146.9 4.3 %collective-permute-start.2 = (f32[16,1024]{1,0:T(8,128)S(1)}, f32[16,1024]{1,0:T(8,128)S(1)}, u32[]{:S(2)}, u32[]{:S(2)}) collective-permute-start(f32[16,1024]{1,0:T(8,128)S(1)} %add.161), channel_id=1, source_target_pairs={{0,8},{2,10},{4,12},{6,14},{8,0},{10,2},{12,4},{14,6},{16,24},{18,... | collective-permute-start | bytes 196616 | tf_op jit(solution)/shard_map/ppermute | solution.py:15
  151.3 5.4 %collective-permute-start.3 = (f32[16,1024]{1,0:T(8,128)S(1)}, f32[16,1024]{1,0:T(8,128)S(1)}, u32[]{:S(2)}, u32[]{:S(2)}) collective-permute-start(f32[16,1024]{1,0:T(8,128)S(1)} %add.162), channel_id=1, source_target_pairs={{0,16},{2,18},{4,20},{6,22},{8,24},{10,26},{12,28},{14,30},{16,0},... | collective-permute-start | bytes 196616 | tf_op jit(solution)/shard_map/ppermute | solution.py:15
Sparse Core Ops, SparseCore 0:
  11.3 63.0 all-gather.1
